TPU v7x, 256 devices: a whole 4x4x8 slice. The times are simulated.
256 devices in a mesh: ab: 16 (over z_lo, y, core), cd: 16 (over z_hi, x).
Axes of the slice: x: 4, y: 4, z: 8 (z_hi: 4, z_lo: 2; z = z_hi * 2 + z_lo), core: 2. Of those that a mesh axis runs over, the one named last changes fastest.
Arguments:
- pair_values: bfloat16 [32768, 32768], P('ab', 'cd'), may hold values from -0.046875 to 0.046875
- amplitudes: bfloat16 [64, 800, 800], P('ab', 'cd'), may hold values from -6 to 6
- cd_first: int32 [32768], P('cd'), may hold values from 0 to 799, as said below
- cd_second: int32 [32768], P('cd'), may hold values from 0 to 799, as said below
- live_cols: int32 [16], P('cd'), may hold values from 512 to 2048, as said below
Outputs:
- ladder: bfloat16 [64, 32768], P(None, ('ab', 'cd'))
Inputs may be any that keep to these rules, and one draw needn't show every extreme that they name: `cd_first`: slot n lies in slab s = n // 2048 and its c lies in orbitals s * 50 to (s + 1) * 50 - 1. cd_second[n] >= cd_first[n] for every slot. `live_cols`: slots 0 and 1 of every slab are live.
All inputs are finite; a program needn't handle non-finite values.
Results may differ from a plain program's by a relative error of at most 0.0051.
Values may be sent and summed in bfloat16 or wider, within the bound.
A program may use at most 64 MiB of HBM per device.

v0:
```python
import jax
import jax.numpy as jnp
from jax import lax
from jax.sharding import PartitionSpec as P


def on_device(pair_values, amplitudes, cd_first, cd_second, live_cols):
    slab = lax.axis_index("cd")
    pair_block = amplitudes.shape[0]
    orbit_block = amplitudes.shape[1]
    orbitals = amplitudes.shape[2]
    columns = cd_first.shape[0]
    local_first = cd_first - slab * orbit_block
    mirrored = lax.all_to_all(amplitudes, "cd", 2, 1, tiled=True)
    pick_d = (lax.broadcasted_iota(jnp.int32, (orbitals, columns), 0) == cd_second[None, :]).astype(
        amplitudes.dtype
    )
    direct_rows = lax.dot_general(
        amplitudes, pick_d, (((2,), (0,)), ((), ())), preferred_element_type=jnp.float32
    )
    crossed_rows = lax.dot_general(
        mirrored, pick_d, (((1,), (0,)), ((), ())), preferred_element_type=jnp.float32
    )
    pick_c = lax.broadcasted_iota(jnp.int32, (orbit_block, columns), 0) == local_first[None, :]
    both = jnp.sum(jnp.where(pick_c[None], direct_rows + crossed_rows, 0.0), axis=1)
    live_count = live_cols[0]
    slots = jnp.arange(columns, dtype=jnp.int32)
    live = (slots < live_count).astype(jnp.float32)
    half = jnp.where(cd_first == cd_second, jnp.float32(0.5), jnp.float32(1.0))
    weight = half * live
    packed = (both * weight[None, :]).astype(jnp.bfloat16)
    contract = (((1,), (1,)), ((), ()))
    partial_sums = lax.dot_general(
        lax.all_gather(packed, "ab", axis=0, tiled=True),
        pair_values,
        contract,
        preferred_element_type=jnp.float32,
    )
    return lax.psum_scatter(partial_sums, "cd", scatter_dimension=1, tiled=True).astype(
        jnp.bfloat16
    )


def solution(mesh):
    placed = (P("ab", "cd"), P("ab", "cd", None), P("cd"), P("cd"), P("cd"))
    return jax.shard_map(
        on_device, mesh=mesh, in_specs=placed, out_specs=P(None, ("ab", "cd")), check_vma=False
    )
```

profile of v0, /device:TPU:8, one launch (start us, length us, event | category | flops | bytes accessed | tf_op | source)
XLA Modules:
  0.0 156.1 jit_solution(14329860062865559062)
XLA Ops:
  6.5 0.0 copy-start.2
  6.5 0.0 copy-start.1
  6.5 2.1 %copy.16 = bf16[4,50,800]{1,0,2:T(4,128)(2,1)S(1)} copy(bf16[4,50,800]{2,0,1:T(4,128)(2,1)} %param.6) | data formatting | bytes 640000 | tf_op args[1]
  8.7 1.8 %reshape.24 = bf16[16,2,5000]{2,1,0:T(2,128)(2,1)} reshape(bf16[800,4,50]{2,1,0:T(4,128)(2,1)S(1)} %bitcast.36) | data formatting | bytes 640000
  10.5 11.0 %all-to-all-start = ((bf16[16,2,5000]{2,1,0:T(2,128)(2,1)}), bf16[16,2,5000]{2,1,0:T(2,128)(2,1)S(1)}, u32[]{:S(2)}, u32[]{:S(2)}) async-start(bf16[16,2,5000]{2,1,0:T(2,128)(2,1)} %reshape.24), calls=%async_computation | async-start | bytes 655360 | tf_op jit(solution)/shard_map/all_to_all | solution.py:14
  21.5 0.0 reduce-scatter.2.cloned.1.call-start
  22.2 0.0 copy-done.2
  22.3 0.0 copy-done.1
  22.3 0.1 iota_compare_fusion.1
  22.4 13.1 %all-to-all-done = bf16[16,2,5000]{2,1,0:T(2,128)(2,1)S(1)} async-done(((bf16[16,2,5000]{2,1,0:T(2,128)(2,1)}), bf16[16,2,5000]{2,1,0:T(2,128)(2,1)S(1)}, u32[]{:S(2)}, u32[]{:S(2)}) %all-to-all-start) | async-done | bytes 320032 | tf_op jit(solution)/shard_map/all_to_all | solution.py:14
  35.5 0.9 reshape.25
  36.4 0.2 copy.24
  36.6 1.2 all_to_all.16
  37.8 0.0 copy-start
  37.8 1.6 %fusion.1 = f32[2048,4,50]{0,2,1:T(8,128)S(1)} fusion(s32[2048]{0:T(1024)S(1)} %copy-done.2, bf16[4,800,50]{1,0,2:T(4,128)(2,1)S(1)} %all_to_all.16), kind=kOutput, calls=%fused_computation.2 | convolution fusion | flops 656998400 | bytes 1966592 | tf_op jit(solution)/shard_map/dot_general | solution.py:21
  39.4 0.0 copy-done
  39.4 1.7 %fusion.16 = f32[4,2048]{1,0:T(4,128)S(1)} fusion(f32[2048,4,50]{0,2,1:T(8,128)S(1)} %fusion.1, s32[2048]{0:T(1024)S(1)} %copy-done.2, pred[50,2048]{1,0:T(8,128)(4,1)S(1)} %iota_compare_fusion.1, bf16[4,50,800]{2,0,1:T(4,128)(2,1)S(1)} %copy-done), kind=kOutput, calls=%fused_computation.9 | convolution fusion | flops 658219008 | bytes 2101760 | tf_op jit(solution)/shard_map/dot_general | solution.py:18
  41.1 17.1 %all-gather = bf16[16,4,2048]{2,1,0:T(4,128)(2,1)S(1)} all-gather(bf16[1,4,2048]{2,1,0:T(4,128)(2,1)S(1)} %fusion.21), channel_id=1, replica_groups=mesh['ab'=16,'cd'=16] {'ab'}, dimensions={0}, use_global_device_ids=true | all-gather | bytes 278528 | tf_op jit(solution)/shard_map/all_gather | solution.py:34
  58.2 0.1 reshape.22
  58.3 6.8 %fusion.22 = f32[64,2048]{1,0:T(8,128)} fusion(bf16[64,2048]{1,0:T(8,128)(2,1)S(1)} %reshape.22, bf16[2048,2048]{1,0:T(8,128)(2,1)} %param.5), kind=kOutput, calls=%fused_computation.19 | convolution fusion | flops 536870912 | bytes 9175040 | tf_op jit(solution)/shard_map/dot_general | solution.py:33
  65.1 0.0 reduce-scatter.2.cloned.1.call-update
  65.1 82.7 %reduce-scatter.2.cloned.1.call-done = f32[64,128]{1,0:T(8,128)} async-done(((f32[64,2048]{1,0:T(8,128)}), f32[64,128]{1,0:T(8,128)}) %reduce-scatter.2.cloned.1.call-update) | async-done | bytes 32784 | tf_op jit(solution)/shard_map/reduce_scatter | solution.py:39
  147.9 1.4 convert_element_type.9
  (3 shorter events, 0.0 us)
Async XLA Ops:
  6.5 15.7 %copy-start.2 = (s32[2048]{0:T(1024)S(1)}, s32[2048]{0:T(1024)}, u32[]{:S(2)}) copy-start(s32[2048]{0:T(1024)} %param.8) | copy-start | bytes 24580
  6.5 15.7 %copy-start.1 = (s32[2048]{0:T(1024)S(1)}, s32[2048]{0:T(1024)}, u32[]{:S(2)}) copy-start(s32[2048]{0:T(1024)} %param.7) | copy-start | bytes 24580
  10.5 25.0 %all-to-all-start = ((bf16[16,2,5000]{2,1,0:T(2,128)(2,1)}), bf16[16,2,5000]{2,1,0:T(2,128)(2,1)S(1)}, u32[]{:S(2)}, u32[]{:S(2)}) async-start(bf16[16,2,5000]{2,1,0:T(2,128)(2,1)} %reshape.24), calls=%async_computation | async-start | bytes 655360 | tf_op jit(solution)/shard_map/all_to_all | solution.py:14
  21.5 126.3 %reduce-scatter.2.cloned.1.call-start = ((), (), s32[]{:S(2)}) async-start(), calls=%async_computation.2 | async-start | bytes 557056 | tf_op jit(solution)/shard_map/reduce_scatter | solution.py:39
  37.8 1.6 %copy-start = (bf16[4,50,800]{2,0,1:T(4,128)(2,1)S(1)}, bf16[4,50,800]{2,0,1:T(4,128)(2,1)}, u32[]{:S(2)}) copy-start(bf16[4,50,800]{2,0,1:T(4,128)(2,1)} %param.6) | copy-start | bytes 960004
Sparse Core Ops, SparseCore 0:
  65.3 82.5 reduce-scatter.1
where the time goes:
time: 156 us
  waiting for transfers between devices  95.9 us (61%)
  blocking collectives  17.1 us (11%)
  between operations  14.2 us (9%)
  starting transfers between devices  11.1 us (7%)
  matrix products  10.1 us (6%)
  local copies, waits for them, and re-layouts  6.28 us (4%)
    reduce_scatter x1, waiting for transfers between devices, on_device(): lax.psum_scatter(partial_sums, 'cd', scatter_dimension=1, tiled=True)  82.7 us
    all_gather x1, blocking collectives, on_device(): lax.all_gather(packed, 'ab', axis=0, tiled=True)  17.1 us
    all_to_all x1, waiting for transfers between devices, on_device(): mirrored = lax.all_to_all(amplitudes, 'cd', 2, 1, tiled=True)  13.1 us
    all_to_all x1, starting transfers between devices, on_device(): mirrored = lax.all_to_all(amplitudes, 'cd', 2, 1, tiled=True)  11 us
    dot_general x1, matrix products, on_device(): lax.dot_general(lax.all_gather(packed, 'ab', axis=0, tiled=True), pair_va...  6.83 us
    unnamed x10, local copies, waits for them, and re-layouts  4.89 us
  transfers between devices with their start and end apart: 2, of which 2 were waited for; matrix products, arithmetic and copies ran while one was open for 0% of the time, Pallas kernels for 0%

commit v1 on v0

--- a/solution.py
+++ b/solution.py
@@ -2,6 +2,15 @@
 import jax.numpy as jnp
 from jax import lax
 from jax.sharding import PartitionSpec as P
+from jax.lax import all_to_all, axis_size
+
+
+def meet_axis_part_by_axis(in_array, mesh_name):
+    z_new = axis_size(mesh_name)
+    s_next = jnp.stack([in_array] * z_new)
+    passed = all_to_all(s_next, mesh_name, 0, 0)
+    part_now = jnp.concatenate(passed, 0)
+    return part_now
 
 
 def on_device(pair_values, amplitudes, cd_first, cd_second, live_cols):
@@ -31,7 +40,7 @@
     packed = (both * weight[None, :]).astype(jnp.bfloat16)
     contract = (((1,), (1,)), ((), ()))
     partial_sums = lax.dot_general(
-        lax.all_gather(packed, "ab", axis=0, tiled=True),
+        meet_axis_part_by_axis(packed, "ab"),
         pair_values,
         contract,
         preferred_element_type=jnp.float32,

time: 156 us -> 149 us (0.955)
  blocking collectives: 17.1 us -> 10.5 us
    all_gather x1 -> x0, blocking collectives: 17.1 us -> none  [on_device(): lax.all_gather(packed, 'ab', axis=0, tiled=True)]
    all_to_all x0 -> x1, blocking collectives: none -> 10.5 us  [meet_axis_part_by_axis(): passed = all_to_all(s_next, mesh_name, 0, 0)]
    unnamed x10 -> x9, local copies, waits for them, and re-layouts: 4.89 us -> 4.83 us
where the time goes in v1:
time: 149 us
  waiting for transfers between devices  95.2 us (64%)
  between operations  14.2 us (10%)
  starting transfers between devices  11.1 us (7%)
  blocking collectives  10.5 us (7%)
  matrix products  10.1 us (7%)
  local copies, waits for them, and re-layouts  6.38 us (4%)
    reduce_scatter x1, waiting for transfers between devices, on_device(): lax.psum_scatter(partial_sums, 'cd', scatter_dimension=1, tiled=True)  82 us
    all_to_all x1, waiting for transfers between devices, on_device(): mirrored = lax.all_to_all(amplitudes, 'cd', 2, 1, tiled=True)  13.1 us
    all_to_all x1, starting transfers between devices, on_device(): mirrored = lax.all_to_all(amplitudes, 'cd', 2, 1, tiled=True)  11 us
    all_to_all x1, blocking collectives, meet_axis_part_by_axis(): passed = all_to_all(s_next, mesh_name, 0, 0)  10.5 us
    dot_general x1, matrix products, on_device(): lax.dot_general(meet_axis_part_by_axis(packed, 'ab'), pair_values, contra...  6.83 us
    unnamed x9, local copies, waits for them, and re-layouts  4.83 us
  transfers between devices with their start and end apart: 2, of which 2 were waited for; matrix products, arithmetic and copies ran while one was open for 0% of the time, Pallas kernels for 0%

profile of v1, /device:TPU:8, one launch (start us, length us, event | category | flops | bytes accessed | tf_op | source)
XLA Modules:
  0.0 148.9 jit_solution(17182092546900442872)
XLA Ops:
  6.5 0.0 copy-start.2
  6.5 0.0 copy-start.1
  6.5 2.1 %copy.16 = bf16[4,50,800]{1,0,2:T(4,128)(2,1)S(1)} copy(bf16[4,50,800]{2,0,1:T(4,128)(2,1)} %param.6) | data formatting | bytes 640000 | tf_op args[1]
  8.7 1.8 %reshape.37 = bf16[16,2,5000]{2,1,0:T(2,128)(2,1)} reshape(bf16[800,4,50]{2,1,0:T(4,128)(2,1)S(1)} %bitcast.34) | data formatting | bytes 640000
  10.5 11.0 %all-to-all-start = ((bf16[16,2,5000]{2,1,0:T(2,128)(2,1)}), bf16[16,2,5000]{2,1,0:T(2,128)(2,1)S(1)}, u32[]{:S(2)}, u32[]{:S(2)}) async-start(bf16[16,2,5000]{2,1,0:T(2,128)(2,1)} %reshape.37), calls=%async_computation | async-start | bytes 655360 | tf_op jit(solution)/shard_map/all_to_all | solution.py:23
  21.5 0.0 reduce-scatter.2.cloned.1.call-start
  22.2 0.0 copy-done.2
  22.3 0.0 copy-done.1
  22.3 0.1 iota_compare_fusion.1
  22.4 13.1 %all-to-all-done = bf16[16,2,5000]{2,1,0:T(2,128)(2,1)S(1)} async-done(((bf16[16,2,5000]{2,1,0:T(2,128)(2,1)}), bf16[16,2,5000]{2,1,0:T(2,128)(2,1)S(1)}, u32[]{:S(2)}, u32[]{:S(2)}) %all-to-all-start) | async-done | bytes 320032 | tf_op jit(solution)/shard_map/all_to_all | solution.py:23
  35.5 0.9 reshape.38
  36.4 0.2 copy.24
  36.6 1.2 all_to_all.19
  37.8 0.0 copy-start
  37.8 1.6 %fusion.1 = f32[2048,4,50]{0,2,1:T(8,128)S(1)} fusion(s32[2048]{0:T(1024)S(1)} %copy-done.2, bf16[4,800,50]{1,0,2:T(4,128)(2,1)S(1)} %all_to_all.19), kind=kOutput, calls=%fused_computation.2 | convolution fusion | flops 656998400 | bytes 1966592 | tf_op jit(solution)/shard_map/dot_general | solution.py:30
  39.4 0.0 copy-done
  39.4 1.7 %fusion.16 = f32[4,2048]{1,0:T(4,128)S(1)} fusion(f32[2048,4,50]{0,2,1:T(8,128)S(1)} %fusion.1, s32[2048]{0:T(1024)S(1)} %copy-done.2, pred[50,2048]{1,0:T(8,128)(4,1)S(1)} %iota_compare_fusion.1, bf16[4,50,800]{2,0,1:T(4,128)(2,1)S(1)} %copy-done), kind=kOutput, calls=%fused_computation.9 | convolution fusion | flops 658219008 | bytes 2101760 | tf_op jit(solution)/shard_map/dot_general | solution.py:27
  41.1 0.1 stack.2
  41.2 10.5 %all_to_all.23 = bf16[16,4,2048]{2,1,0:T(4,128)(2,1)S(1)} all-to-all(bf16[16,4,2048]{2,1,0:T(4,128)(2,1)S(1)} %stack.2), channel_id=1, replica_groups=mesh['ab'=16,'cd'=16] {'ab'}, dimensions={0} | all-to-all | bytes 524288 | tf_op jit(solution)/shard_map/all_to_all | solution.py:11
  51.8 0.1 reshape.35
  51.8 6.8 %fusion.21 = f32[64,2048]{1,0:T(8,128)} fusion(bf16[64,2048]{1,0:T(8,128)(2,1)S(1)} %reshape.35, bf16[2048,2048]{1,0:T(8,128)(2,1)} %param.5), kind=kOutput, calls=%fused_computation.18 | convolution fusion | flops 536870912 | bytes 9175040 | tf_op jit(solution)/shard_map/dot_general | solution.py:42
  58.7 0.0 reduce-scatter.2.cloned.1.call-update
  58.7 82.0 %reduce-scatter.2.cloned.1.call-done = f32[64,128]{1,0:T(8,128)} async-done(((f32[64,2048]{1,0:T(8,128)}), f32[64,128]{1,0:T(8,128)}) %reduce-scatter.2.cloned.1.call-update) | async-done | bytes 32784 | tf_op jit(solution)/shard_map/reduce_scatter | solution.py:48
  140.7 1.4 convert_element_type.11
  (3 shorter events, 0.0 us)
Async XLA Ops:
  6.5 15.7 %copy-start.2 = (s32[2048]{0:T(1024)S(1)}, s32[2048]{0:T(1024)}, u32[]{:S(2)}) copy-start(s32[2048]{0:T(1024)} %param.8) | copy-start | bytes 24580
  6.5 15.7 %copy-start.1 = (s32[2048]{0:T(1024)S(1)}, s32[2048]{0:T(1024)}, u32[]{:S(2)}) copy-start(s32[2048]{0:T(1024)} %param.7) | copy-start | bytes 24580
  10.5 25.0 %all-to-all-start = ((bf16[16,2,5000]{2,1,0:T(2,128)(2,1)}), bf16[16,2,5000]{2,1,0:T(2,128)(2,1)S(1)}, u32[]{:S(2)}, u32[]{:S(2)}) async-start(bf16[16,2,5000]{2,1,0:T(2,128)(2,1)} %reshape.37), calls=%async_computation | async-start | bytes 655360 | tf_op jit(solution)/shard_map/all_to_all | solution.py:23
  21.5 119.1 %reduce-scatter.2.cloned.1.call-start = ((), (), s32[]{:S(2)}) async-start(), calls=%async_computation.3 | async-start | bytes 557056 | tf_op jit(solution)/shard_map/reduce_scatter | solution.py:48
  37.8 1.6 %copy-start = (bf16[4,50,800]{2,0,1:T(4,128)(2,1)S(1)}, bf16[4,50,800]{2,0,1:T(4,128)(2,1)}, u32[]{:S(2)}) copy-start(bf16[4,50,800]{2,0,1:T(4,128)(2,1)} %param.6) | copy-start | bytes 960004
Sparse Core Ops, SparseCore 0:
  58.8 81.8 reduce-scatter.1
